TPU v7x, 32 devices: a whole 2x2x4 slice. The times are simulated.
32 devices in a mesh: batch: 8 (over z, y), tensor: 4 (over x, core).
Axes of the slice: x: 2, y: 2, z: 4, core: 2. Of those that a mesh axis runs over, the one named last changes fastest.
Arguments:
- maps_five: bfloat16 [2, 48, 5, 5, 2048], P(None, 'batch', None, None, 'tensor'), may hold values from -6 to 6
- maps_seven: bfloat16 [2, 48, 7, 7, 2048], P(None, 'batch', None, None, 'tensor'), may hold values from -6 to 6
- maps_nine: bfloat16 [2, 24, 9, 9, 2048], P(None, 'batch', None, None, 'tensor'), may hold values from -6 to 6
- upstream_five: bfloat16 [2, 48, 5, 5, 2048], P(None, 'batch', None, None, 'tensor'), may hold values from -6 to 6
- upstream_seven: bfloat16 [2, 48, 7, 7, 2048], P(None, 'batch', None, None, 'tensor'), may hold values from -6 to 6
- upstream_nine: bfloat16 [2, 24, 9, 9, 2048], P(None, 'batch', None, None, 'tensor'), may hold values from -6 to 6
- reduce_weight: bfloat16 [2048, 1024], P(None, 'tensor'), may hold values from -0.125 to 0.125
- group_weight: bfloat16 [3, 3, 32, 32, 32], P(None, None, 'tensor'), may hold values from -0.375 to 0.375
- expand_weight: bfloat16 [1024, 2048], P('tensor'), may hold values from -0.1875 to 0.1875
- first_gain: float32 [1024], P('tensor'), may hold values from 0.25 to 1.75
- first_bias: float32 [1024], P('tensor'), may hold values from -3 to 3
- second_gain: float32 [1024], P('tensor'), may hold values from 0.25 to 1.75
- second_bias: float32 [1024], P('tensor'), may hold values from -3 to 3
- third_gain: float32 [2048], P('tensor'), may hold values from 0.25 to 1.75
- third_bias: float32 [2048], P('tensor'), may hold values from -3 to 3
- image_counts: int32 [2, 8, 3], P(None, 'batch'), may hold values from 0 to 6, as said below
Outputs:
- result_five: bfloat16 [2, 48, 5, 5, 2048], P(None, 'batch', None, None, 'tensor')
- result_seven: bfloat16 [2, 48, 7, 7, 2048], P(None, 'batch', None, None, 'tensor')
- result_nine: bfloat16 [2, 24, 9, 9, 2048], P(None, 'batch', None, None, 'tensor')
- backprop_five: float32 [2, 48, 5, 5, 2048], P(None, 'batch', None, None, 'tensor')
- backprop_seven: float32 [2, 48, 7, 7, 2048], P(None, 'batch', None, None, 'tensor')
- backprop_nine: float32 [2, 24, 9, 9, 2048], P(None, 'batch', None, None, 'tensor')
- reduce_grad: float32 [2048, 1024], P(None, 'tensor')
- group_grad: float32 [3, 3, 32, 32, 32], P(None, None, 'tensor')
- expand_grad: float32 [1024, 2048], P('tensor')
- first_gain_grad: float32 [1024], P('tensor')
- first_bias_grad: float32 [1024], P('tensor')
- second_gain_grad: float32 [1024], P('tensor')
- second_bias_grad: float32 [1024], P('tensor')
- third_gain_grad: float32 [2048], P('tensor')
- third_bias_grad: float32 [2048], P('tensor')
Inputs may be any that keep to these rules, and one draw needn't show every extreme that they name: image_counts[m, b, r] is the number of live images of resolution r (5x5, 7x7, 9x9) on rank b in micro-batch m, at most 6, 6, 3 for r = 0, 1, 2; a rank's live images fill its first slots; for every micro-batch and resolution some rank holds the most.
All inputs are finite; a program needn't handle non-finite values.
Results may differ from a plain program's by a relative error of at most 0.0095.
Values may be sent and summed in bfloat16 or wider, within the bound.
No kernel may reach another device: no remote copies, remote signals or barrier semaphores. Data moves between devices by JAX's collectives and lax.ppermute only.
A program may use at most 192 MiB of HBM per device.

v0:
```python
import jax
import jax.numpy as jnp
from jax import lax
from jax.sharding import PartitionSpec as P

EPSILON = 1e-05


def slope(values):
    sigmoid_value = jax.nn.sigmoid(values)
    return sigmoid_value * (1.0 + values * (1.0 - sigmoid_value))


def normed_parts(values, sums, squares, pixel_total):
    mean_value = sums / pixel_total
    variance = squares / pixel_total - mean_value * mean_value
    inverse = lax.rsqrt(variance + EPSILON)
    return ((values - mean_value) * inverse, inverse)


def norm_back(grad_pre, normed, inverse, gain, live_mask, pixel_total, grad_sum, grad_cross):
    return inverse * gain * (grad_pre - live_mask * (grad_sum + normed * grad_cross) / pixel_total)


def padded_blocks(flat, edges, slot_list):
    channel_count = flat.shape[1]
    offset = 0
    found = []
    for edge_size, slot_count in zip(edges, slot_list):
        pixel_count = slot_count * edge_size * edge_size
        blocks = flat[offset : offset + pixel_count].reshape(
            slot_count, edge_size, edge_size, channel_count
        )
        found.append(jnp.pad(blocks, ((0, 0), (1, 1), (1, 1), (0, 0))))
        offset = offset + pixel_count
    return found


def tap_conv(flat, matrices, edges, slot_list):
    channel_count = flat.shape[1]
    pieces = []
    for padded, edge_size, slot_count in zip(
        padded_blocks(flat, edges, slot_list), edges, slot_list
    ):
        pixel_count = slot_count * edge_size * edge_size
        summed = jnp.zeros((pixel_count, matrices.shape[2]), jnp.float32)
        for tap_index in range(9):
            row_start = tap_index // 3
            col_start = tap_index % 3
            window = padded[
                :, row_start : row_start + edge_size, col_start : col_start + edge_size, :
            ].reshape(pixel_count, channel_count)
            summed = summed + jnp.dot(
                window, matrices[tap_index], preferred_element_type=jnp.float32
            )
        pieces.append(summed)
    return jnp.concatenate(pieces, 0)


def kernel_grad(flat, grad_flat, edges, slot_list, group_count, group_width):
    collected = jnp.zeros((9, group_count, group_width, group_width), jnp.float32)
    offset = 0
    for padded, edge_size, slot_count in zip(
        padded_blocks(flat, edges, slot_list), edges, slot_list
    ):
        pixel_count = slot_count * edge_size * edge_size
        grad_part = grad_flat[offset : offset + pixel_count].reshape(
            pixel_count, group_count, group_width
        )
        taps_list = []
        for tap_index in range(9):
            row_start = tap_index // 3
            col_start = tap_index % 3
            window = padded[
                :, row_start : row_start + edge_size, col_start : col_start + edge_size, :
            ].reshape(pixel_count, group_count, group_width)
            taps_list.append(
                jnp.einsum("pgi,pgo->gio", window, grad_part, preferred_element_type=jnp.float32)
            )
        collected = collected + jnp.stack(taps_list, 0)
        offset = offset + pixel_count
    return collected.reshape(3, 3, group_count, group_width, group_width)


def split_back(flat, edges, slot_list, channel_count):
    found = []
    offset = 0
    for edge_size, slot_count in zip(edges, slot_list):
        pixel_count = slot_count * edge_size * edge_size
        found.append(
            flat[offset : offset + pixel_count].reshape(
                slot_count, edge_size, edge_size, channel_count
            )
        )
        offset = offset + pixel_count
    return found


def per_device(
    maps_five,
    maps_seven,
    maps_nine,
    upstream_five,
    upstream_seven,
    upstream_nine,
    reduce_weight,
    group_weight,
    expand_weight,
    first_gain,
    first_bias,
    second_gain,
    second_bias,
    third_gain,
    third_bias,
    image_counts,
):
    all_maps = (maps_five, maps_seven, maps_nine)
    all_upstream = (upstream_five, upstream_seven, upstream_nine)
    edges = tuple((piece.shape[2] for piece in all_maps))
    slot_list = tuple((piece.shape[1] for piece in all_maps))
    micro_count = maps_five.shape[0]
    chan_local = maps_five.shape[-1]
    group_count = group_weight.shape[2]
    group_width = group_weight.shape[3]
    inner_local = group_count * group_width
    identity = jnp.eye(group_count, dtype=jnp.bfloat16)
    matrices = jnp.einsum("abgio,gh->abgiho", group_weight, identity).reshape(
        9, inner_local, inner_local
    )
    matrices_back = jnp.transpose(jnp.flip(matrices, 0), (0, 2, 1))
    expand_cols = lax.all_to_all(expand_weight, "tensor", split_axis=1, concat_axis=0, tiled=True)
    reduce_rows = lax.all_to_all(reduce_weight, "tensor", split_axis=0, concat_axis=1, tiled=True)
    reduce_acc = jnp.zeros(reduce_weight.shape, jnp.float32)
    group_acc = jnp.zeros(group_weight.shape, jnp.float32)
    expand_acc = jnp.zeros(expand_weight.shape, jnp.float32)
    gain_one_acc = jnp.zeros_like(first_gain)
    bias_one_acc = jnp.zeros_like(first_bias)
    gain_two_acc = jnp.zeros_like(second_gain)
    bias_two_acc = jnp.zeros_like(second_bias)
    gain_three_acc = jnp.zeros_like(third_gain)
    bias_three_acc = jnp.zeros_like(third_bias)
    results = [[], [], []]
    backs = [[], [], []]
    for step_index in range(micro_count):
        local_maps = jnp.concatenate(
            [piece[step_index].reshape(-1, chan_local) for piece in all_maps], 0
        )
        counts_now = image_counts[step_index, 0]
        mask_pieces = []
        local_pixels = jnp.float32(0.0)
        for column in range(3):
            live = (jnp.arange(slot_list[column], dtype=jnp.int32) < counts_now[column]).astype(
                jnp.float32
            )
            mask_pieces.append(jnp.repeat(live, edges[column] * edges[column]))
            local_pixels = local_pixels + (
                counts_now[column] * edges[column] * edges[column]
            ).astype(jnp.float32)
        live_mask = jnp.concatenate(mask_pieces, 0)[:, None]
        full_maps = lax.all_gather(local_maps, "tensor", axis=1, tiled=True)
        first = jnp.dot(full_maps, reduce_weight, preferred_element_type=jnp.float32)
        sum_one, square_one, pixel_total = lax.psum(
            (jnp.sum(live_mask * first, 0), jnp.sum(live_mask * first * first, 0), local_pixels),
            "batch",
        )
        normed_one, inverse_one = normed_parts(first, sum_one, square_one, pixel_total)
        pre_one = first_gain * normed_one + first_bias
        act_one = (live_mask * jax.nn.silu(pre_one)).astype(jnp.bfloat16)
        second = tap_conv(act_one, matrices, edges, slot_list)
        sum_two, square_two = lax.psum(
            (jnp.sum(live_mask * second, 0), jnp.sum(live_mask * second * second, 0)), "batch"
        )
        normed_two, inverse_two = normed_parts(second, sum_two, square_two, pixel_total)
        pre_two = second_gain * normed_two + second_bias
        act_two = (live_mask * jax.nn.silu(pre_two)).astype(jnp.bfloat16)
        third = jnp.dot(
            lax.all_gather(act_two, "tensor", axis=1, tiled=True),
            expand_cols,
            preferred_element_type=jnp.float32,
        )
        sum_three, square_three = lax.psum(
            (jnp.sum(live_mask * third, 0), jnp.sum(live_mask * third * third, 0)), "batch"
        )
        normed_three, inverse_three = normed_parts(third, sum_three, square_three, pixel_total)
        pre_three = third_gain * normed_three + third_bias + local_maps.astype(jnp.float32)
        output = (live_mask * jax.nn.silu(pre_three)).astype(jnp.bfloat16)
        upstream = jnp.concatenate(
            [piece[step_index].reshape(-1, chan_local) for piece in all_upstream], 0
        ).astype(jnp.float32)
        grad_pre_three = live_mask * upstream * slope(pre_three)
        sum_g_three, cross_three = lax.psum(
            (jnp.sum(grad_pre_three, 0), jnp.sum(grad_pre_three * normed_three, 0)), "batch"
        )
        bias_three_acc = bias_three_acc + sum_g_three
        gain_three_acc = gain_three_acc + cross_three
        grad_third = norm_back(
            grad_pre_three,
            normed_three,
            inverse_three,
            third_gain,
            live_mask,
            pixel_total,
            sum_g_three,
            cross_three,
        ).astype(jnp.bfloat16)
        full_grad = lax.all_gather(grad_third, "tensor", axis=1, tiled=True)
        expand_step = lax.dot_general(
            act_two, full_grad, (((0,), (0,)), ((), ())), preferred_element_type=jnp.float32
        )
        grad_act_two = lax.dot_general(
            full_grad, expand_weight, (((1,), (1,)), ((), ())), preferred_element_type=jnp.float32
        )
        grad_pre_two = live_mask * grad_act_two * slope(pre_two)
        sum_g_two, cross_two = lax.psum(
            (jnp.sum(grad_pre_two, 0), jnp.sum(grad_pre_two * normed_two, 0)), "batch"
        )
        bias_two_acc = bias_two_acc + sum_g_two
        gain_two_acc = gain_two_acc + cross_two
        grad_second = norm_back(
            grad_pre_two,
            normed_two,
            inverse_two,
            second_gain,
            live_mask,
            pixel_total,
            sum_g_two,
            cross_two,
        ).astype(jnp.bfloat16)
        group_step = kernel_grad(act_one, grad_second, edges, slot_list, group_count, group_width)
        grad_act_one = tap_conv(grad_second, matrices_back, edges, slot_list)
        grad_pre_one = live_mask * grad_act_one * slope(pre_one)
        sum_g_one, cross_one = lax.psum(
            (jnp.sum(grad_pre_one, 0), jnp.sum(grad_pre_one * normed_one, 0)), "batch"
        )
        bias_one_acc = bias_one_acc + sum_g_one
        gain_one_acc = gain_one_acc + cross_one
        grad_first = norm_back(
            grad_pre_one,
            normed_one,
            inverse_one,
            first_gain,
            live_mask,
            pixel_total,
            sum_g_one,
            cross_one,
        ).astype(jnp.bfloat16)
        reduce_step = lax.dot_general(
            full_maps, grad_first, (((0,), (0,)), ((), ())), preferred_element_type=jnp.float32
        )
        back_local = lax.dot_general(
            lax.all_gather(grad_first, "tensor", axis=1, tiled=True),
            reduce_rows,
            (((1,), (1,)), ((), ())),
            preferred_element_type=jnp.float32,
        )
        backprop = grad_pre_three + back_local
        reduce_acc = reduce_acc + reduce_step
        group_acc = group_acc + group_step
        expand_acc = expand_acc + expand_step
        for column, piece in enumerate(split_back(output, edges, slot_list, chan_local)):
            results[column].append(piece)
        for column, piece in enumerate(split_back(backprop, edges, slot_list, chan_local)):
            backs[column].append(piece)
    reduce_acc, group_acc, expand_acc = lax.psum((reduce_acc, group_acc, expand_acc), "batch")
    stacked = [jnp.stack(results[column], 0) for column in range(3)]
    grads_in = [jnp.stack(backs[column], 0) for column in range(3)]
    return (
        stacked[0],
        stacked[1],
        stacked[2],
        grads_in[0],
        grads_in[1],
        grads_in[2],
        reduce_acc,
        group_acc,
        expand_acc,
        gain_one_acc,
        bias_one_acc,
        gain_two_acc,
        bias_two_acc,
        gain_three_acc,
        bias_three_acc,
    )


def solution(mesh):
    in_specs = (
        P(None, "batch", None, None, "tensor"),
        P(None, "batch", None, None, "tensor"),
        P(None, "batch", None, None, "tensor"),
        P(None, "batch", None, None, "tensor"),
        P(None, "batch", None, None, "tensor"),
        P(None, "batch", None, None, "tensor"),
        P(None, "tensor"),
        P(None, None, "tensor", None, None),
        P("tensor", None),
        P("tensor"),
        P("tensor"),
        P("tensor"),
        P("tensor"),
        P("tensor"),
        P("tensor"),
        P(None, "batch", None),
    )
    out_specs = (
        P(None, "batch", None, None, "tensor"),
        P(None, "batch", None, None, "tensor"),
        P(None, "batch", None, None, "tensor"),
        P(None, "batch", None, None, "tensor"),
        P(None, "batch", None, None, "tensor"),
        P(None, "batch", None, None, "tensor"),
        P(None, "tensor"),
        P(None, None, "tensor", None, None),
        P("tensor", None),
        P("tensor"),
        P("tensor"),
        P("tensor"),
        P("tensor"),
        P("tensor"),
        P("tensor"),
    )
    return jax.shard_map(
        per_device, mesh=mesh, in_specs=in_specs, out_specs=out_specs, check_vma=False
    )
```

profile of v0, /device:TPU:0, one launch (start us, length us, event | category | flops | bytes accessed | tf_op | source)
XLA Modules:
  0.0 804.1 jit_solution(13690166309197781689)
XLA Ops:
  7.2 3.5 slice_reduce_fusion.7
  10.9 2.6 slice_reduce_fusion.3
  27.0 2.8 multiply_bitcast_fusion
  29.8 5.8 reshape.665
  35.7 9.9 %all-gather.9.cloned.1.call-done = bf16[687,2048]{1,0:T(8,128)(2,1)} async-done(((bf16[687,512]{1,0:T(8,128)(2,1)}), bf16[687,2048]{1,0:T(8,128)(2,1)}) %all-gather.9.cloned.1.call-update) | async-done | bytes 2813968 | tf_op jit(solution)/shard_map/all_gather | solution.py:160
  45.6 3.0 fusion.58
  48.6 25.9 %all-gather.13.cloned.1.call-done = bf16[687,2048]{1,0:T(8,128)(2,1)} async-done(((bf16[687,512]{1,0:T(8,128)(2,1)}), bf16[687,2048]{1,0:T(8,128)(2,1)}) %all-gather.13.cloned.1.call-update) | async-done | bytes 2813968 | tf_op jit(solution)/shard_map/all_gather | solution.py:160
  74.5 3.0 fusion.60
  77.5 22.4 %all-reduce.17 = (f32[256]{0:T(256)S(1)}, f32[]{:T(128)}, f32[256]{0:T(256)S(1)}, f32[256]{0:T(256)S(1)}, f32[]{:T(128)}, /*index=5*/f32[256]{0:T(256)S(1)}) all-reduce(f32[256]{0:T(256)S(1)} %get-tuple-element.60, f32[]{:T(128)S(6)} %add.636, f32[256]{0:T(256)S(1)} %get-tuple-element.59, ...), channel_id=1, replica_groups=mesh['batch'=8,'tensor'=4] {'batch'}, use_global_device_ids=true, to_apply=%region_14.15 | all-reduce | flops 1026 | bytes 8208 | tf_op jit(solution)/shard_map/psum | solution.py:162
  105.9 2.4 pad_slice_fusion.88
  120.7 2.9 pad_slice_fusion.24
  138.5 3.3 pad_slice_fusion.56
  165.3 2.8 pad_slice_fusion.16
  181.2 3.3 pad_slice_fusion.48
  203.9 17.5 %all-reduce.16 = (f32[256]{0:T(256)S(1)}, f32[256]{0:T(256)S(1)}, f32[256]{0:T(256)S(1)}, f32[256]{0:T(256)S(1)}) all-reduce(f32[256]{0:T(256)S(1)} %get-tuple-element.56, f32[256]{0:T(256)S(1)} %get-tuple-element.55, f32[256]{0:T(256)S(1)} %get-tuple-element.54, ...), channel_id=1, replica_groups=mesh['batch'=8,'tensor'=4] {'batch'}, use_global_device_ids=true, to_apply=%region_19.20 | all-reduce | flops 1024 | bytes 8192 | tf_op jit(solution)/shard_map/psum | solution.py:170
  225.5 2.3 copy.219
  227.8 3.5 all-to-all-start
  231.4 4.3 slice_reduce_fusion.5
  239.4 4.7 slice_reduce_fusion.1
  246.7 3.1 slice_reduce_fusion.9
  253.5 3.7 multiply_reduce_fusion.1
  257.3 12.4 %all-gather.15.cloned.1.call-done = bf16[687,1024]{1,0:T(8,128)(2,1)} async-done(((bf16[687,256]{1,0:T(8,128)(2,1)}), bf16[687,1024]{1,0:T(8,128)(2,1)}) %all-gather.15.cloned.1.call-update) | async-done | bytes 1406992 | tf_op jit(solution)/shard_map/all_gather | solution.py:177
  269.6 3.3 multiply_reduce_fusion
  273.0 21.6 %all-reduce.15 = (f32[512]{0:T(512)S(1)}, f32[512]{0:T(512)S(1)}, f32[512]{0:T(512)S(1)}, f32[512]{0:T(512)S(1)}) all-reduce(f32[512]{0:T(512)S(1)} %get-tuple-element.48, f32[512]{0:T(512)S(1)} %get-tuple-element.47, f32[512]{0:T(512)S(1)} %get-tuple-element.46, ...), channel_id=1, replica_groups=mesh['batch'=8,'tensor'=4] {'batch'}, use_global_device_ids=true, to_apply=%region_25.26 | all-reduce | flops 2048 | bytes 16384 | tf_op jit(solution)/shard_map/psum | solution.py:181
  296.6 9.4 %fusion.137 = (f32[512]{0:T(512)}, f32[512]{0:T(512)}, f32[687,512]{1,0:T(8,128)}, bf16[687,512]{1,0:T(8,128)(2,1)}, bf16[687,512]{1,0:T(8,128)(2,1)}, /*index=5...) fusion(f32[512]{0:T(512)S(1)} %get-tuple-element.125, f32[687,512]{1,0:T(8,128)} %get-tuple-element.258, ...), kind=kLoop, calls=%fused_computation.511 | loop fusion | flops 22509568 | bytes 9874808 | tf_op jit(solution)/shard_map/reduce_sum | solution.py:192
  306.0 18.1 %all-reduce.14 = (f32[512]{0:T(512)}, f32[512]{0:T(512)}, f32[512]{0:T(512)}, f32[512]{0:T(512)}) all-reduce(f32[512]{0:T(512)} %get-tuple-element.229, f32[512]{0:T(512)} %get-tuple-element.230, f32[512]{0:T(512)} %get-tuple-element.50, f32[512]{0:T(512)} %get-tuple-element.49), channel_id=1, replica_groups=mesh['batch'=8,'tensor'=4] {'batch'}, use_global_device_ids=true, to_apply=%region_41.42 | all-reduce | flops 2048 | bytes 16384 | tf_op jit(solution)/shard_map/psum | solution.py:191
  324.1 3.3 multiply_convert_fusion
  327.5 3.7 multiply_convert_fusion.1
  331.6 2.2 reshape.785
  333.8 2.2 reshape.787
  385.0 2.1 reshape.832
  389.5 4.2 fusion.142
  393.7 4.1 fusion.140
  397.8 19.7 %all-reduce.13 = (f32[256]{0:T(256)}, f32[256]{0:T(256)}, f32[256]{0:T(256)S(1)}, f32[256]{0:T(256)S(1)}) all-reduce(f32[256]{0:T(256)S(1)} %get-tuple-element.68, f32[256]{0:T(256)S(1)} %get-tuple-element.67, f32[256]{0:T(256)S(1)} %get-tuple-element.64, f32[256]{0:T(256)S(1)} %get-tuple-element.63), channel_id=1, replica_groups=mesh['batch'=8,'tensor'=4] {'batch'}, use_global_device_ids=true, to_apply=%region_45.46 | all-reduce | flops 1024 | bytes 8192 | tf_op jit(solution)/shard_map/psum | solution.py:214
  417.5 2.1 multiply_convert_fusion.7
  500.2 3.2 pad_slice_fusion.40
  530.7 17.3 %all-reduce.12 = (f32[256]{0:T(256)S(1)}, f32[256]{0:T(256)S(1)}, f32[256]{0:T(256)S(1)}, f32[256]{0:T(256)S(1)}) all-reduce(f32[256]{0:T(256)S(1)} %get-tuple-element.232, f32[256]{0:T(256)S(1)} %get-tuple-element.233, f32[256]{0:T(256)S(1)} %get-tuple-element.62, ...), channel_id=1, replica_groups=mesh['batch'=8,'tensor'=4] {'batch'}, use_global_device_ids=true, to_apply=%region_49.50 | all-reduce | flops 1024 | bytes 8192 | tf_op jit(solution)/shard_map/psum | solution.py:232
  581.6 2.9 fusion.153
  586.7 2.3 convolution_add_fusion
  589.1 2.4 convolution_add_fusion.1
  592.5 3.2 add_add_fusion
  596.9 16.9 %all_to_all.38 = bf16[4,512,256]{2,1,0:T(8,128)(2,1)S(1)} all-to-all(bf16[4,512,256]{2,1,0:T(8,128)(2,1)S(1)} %bitcast.594), channel_id=1, replica_groups=mesh['batch'=8,'tensor'=4] {'tensor'}, dimensions={0} | all-to-all | bytes 2097152 | tf_op jit(solution)/shard_map/all_to_all | solution.py:132
  620.1 2.2 pad_maximum_fusion.8
  624.5 2.5 convolution_add_fusion.3
  628.9 2.5 convolution_add_fusion.2
  637.8 2.0 copy.287
  641.4 149.5 %all-reduce.21.cloned.1.call-done = (f32[2048,256]{1,0:T(8,128)}, f32[3,3,8,32,32]{4,3,2,1,0:T(8,128)}, f32[256,2048]{1,0:T(8,128)}) async-done(((f32[2048,256]{1,0:T(8,128)}, f32[3,3,8,32,32]{4,3,2,1,0:T(8,128)}, f32[256,2048]{1,0:T(8,128)}), (f32[2048,256]{1,0:T(8,128)}, f32[3,3,8,32,32]{4,3,2,1,0:T(8,128)}, f32[256,2048]{1,0:T(8,128)})) %all-reduce.21.cloned.1.call-update) | async-done | bytes 4489232 | tf_op jit(solution)/shard_map/psum | solution.py:264
  790.9 3.1 copy.448
  (1089 shorter events, 331.4 us)
Async XLA Ops:
  7.2 38.4 %all-gather.9.cloned.1.call-start = ((), (), s32[]{:S(2)}) async-start(), calls=%async_computation.2 | async-start | bytes 3522560 | tf_op jit(solution)/shard_map/all_gather | solution.py:160
  16.1 58.4 %all-gather.13.cloned.1.call-start = ((), (), s32[]{:S(2)}) async-start(), calls=%async_computation.4 | async-start | bytes 3522560 | tf_op jit(solution)/shard_map/all_gather | solution.py:160
  16.5 10.5 %copy-start.85 = (bf16[150,512]{1,0:T(8,128)(2,1)}, bf16[150,512]{1,0:T(8,128)(2,1)S(1)}, u32[]{:S(2)}) copy-start(bf16[150,512]{1,0:T(8,128)(2,1)S(1)} %reshape_squeeze.39) | copy-start | bytes 460804
  16.5 10.5 %copy-start.209 = (bf16[3,3,8,32,32]{4,3,2,1,0:T(8,128)(2,1)S(1)}, bf16[3,3,8,32,32]{4,3,2,1,0:T(8,128)(2,1)}, u32[]{:S(2)}) copy-start(bf16[3,3,8,32,32]{4,3,2,1,0:T(8,128)(2,1)} %param.23) | copy-start | bytes 442372
  17.5 236.0 %all-gather.11.cloned.1.call-start = ((), (), s32[]{:S(2)}) async-start(), calls=%async_computation.3 | async-start | bytes 1761280 | tf_op jit(solution)/shard_map/all_gather | solution.py:177
  48.6 53.2 %copy-start.1 = (f32[687,256]{1,0:T(8,128)}, f32[687,256]{1,0:T(8,128)S(1)}, u32[]{:S(2)}) copy-start(f32[687,256]{1,0:T(8,128)S(1)} %get-tuple-element.256) | copy-start | bytes 2110468
  74.5 25.4 %copy-start.287 = (f32[256]{0:T(256)S(1)}, f32[256]{0:T(256)}, u32[]{:S(2)}) copy-start(f32[256]{0:T(256)} %param.25) | copy-start | bytes 3076
  74.5 27.4 %copy-start.308 = (f32[256]{0:T(256)S(1)}, f32[256]{0:T(256)}, u32[]{:S(2)}) copy-start(f32[256]{0:T(256)} %param.26) | copy-start | bytes 3076
  102.5 17.5 %copy-start.88 = (bf16[294,256]{1,0:T(8,128)(2,1)}, bf16[294,256]{1,0:T(8,128)(2,1)S(1)}, u32[]{:S(2)}) copy-start(bf16[294,256]{1,0:T(8,128)(2,1)S(1)} %slice.822) | copy-start | bytes 451588
  108.3 9.6 %copy-start.126 = (bf16[6,5,5,256]{3,2,1,0:T(8,128)(2,1)}, bf16[6,5,5,256]{3,2,1,0:T(8,128)(2,1)S(1)}, u32[]{:S(2)}) copy-start(bf16[6,5,5,256]{3,2,1,0:T(8,128)(2,1)S(1)} %get-tuple-element.217) | copy-start | bytes 230404
  108.4 10.3 %copy-start.124 = (bf16[6,5,5,256]{3,2,1,0:T(8,128)(2,1)}, bf16[6,5,5,256]{3,2,1,0:T(8,128)(2,1)S(1)}, u32[]{:S(2)}) copy-start(bf16[6,5,5,256]{3,2,1,0:T(8,128)(2,1)S(1)} %get-tuple-element.218) | copy-start | bytes 230404
  108.4 11.0 %copy-start.122 = (bf16[6,5,5,256]{3,2,1,0:T(8,128)(2,1)}, bf16[6,5,5,256]{3,2,1,0:T(8,128)(2,1)S(1)}, u32[]{:S(2)}) copy-start(bf16[6,5,5,256]{3,2,1,0:T(8,128)(2,1)S(1)} %get-tuple-element.212) | copy-start | bytes 230404
  123.6 11.3 %copy-start.61 = (bf16[6,7,7,256]{3,2,1,0:T(8,128)(2,1)}, bf16[6,7,7,256]{3,2,1,0:T(8,128)(2,1)S(1)}, u32[]{:S(2)}) copy-start(bf16[6,7,7,256]{3,2,1,0:T(8,128)(2,1)S(1)} %get-tuple-element.184) | copy-start | bytes 451588
  123.6 12.0 %copy-start.59 = (bf16[6,7,7,256]{3,2,1,0:T(8,128)(2,1)}, bf16[6,7,7,256]{3,2,1,0:T(8,128)(2,1)S(1)}, u32[]{:S(2)}) copy-start(bf16[6,7,7,256]{3,2,1,0:T(8,128)(2,1)S(1)} %get-tuple-element.185) | copy-start | bytes 451588
  123.6 12.7 %copy-start.57 = (bf16[6,7,7,256]{3,2,1,0:T(8,128)(2,1)}, bf16[6,7,7,256]{3,2,1,0:T(8,128)(2,1)S(1)}, u32[]{:S(2)}) copy-start(bf16[6,7,7,256]{3,2,1,0:T(8,128)(2,1)S(1)} %get-tuple-element.186) | copy-start | bytes 451588
  123.7 13.4 %copy-start.55 = (bf16[6,7,7,256]{3,2,1,0:T(8,128)(2,1)}, bf16[6,7,7,256]{3,2,1,0:T(8,128)(2,1)S(1)}, u32[]{:S(2)}) copy-start(bf16[6,7,7,256]{3,2,1,0:T(8,128)(2,1)S(1)} %get-tuple-element.180) | copy-start | bytes 451588
  141.8 12.1 %copy-start.37 = (bf16[3,9,9,256]{3,2,1,0:T(8,128)(2,1)}, bf16[3,9,9,256]{3,2,1,0:T(8,128)(2,1)S(1)}, u32[]{:S(2)}) copy-start(bf16[3,9,9,256]{3,2,1,0:T(8,128)(2,1)S(1)} %get-tuple-element.152) | copy-start | bytes 373252
  141.8 12.8 %copy-start.35 = (bf16[3,9,9,256]{3,2,1,0:T(8,128)(2,1)}, bf16[3,9,9,256]{3,2,1,0:T(8,128)(2,1)S(1)}, u32[]{:S(2)}) copy-start(bf16[3,9,9,256]{3,2,1,0:T(8,128)(2,1)S(1)} %get-tuple-element.153) | copy-start | bytes 373252
  141.8 13.6 %copy-start.33 = (bf16[3,9,9,256]{3,2,1,0:T(8,128)(2,1)}, bf16[3,9,9,256]{3,2,1,0:T(8,128)(2,1)S(1)}, u32[]{:S(2)}) copy-start(bf16[3,9,9,256]{3,2,1,0:T(8,128)(2,1)S(1)} %get-tuple-element.154) | copy-start | bytes 373252
  141.8 14.3 %copy-start.31 = (bf16[3,9,9,256]{3,2,1,0:T(8,128)(2,1)}, bf16[3,9,9,256]{3,2,1,0:T(8,128)(2,1)S(1)}, u32[]{:S(2)}) copy-start(bf16[3,9,9,256]{3,2,1,0:T(8,128)(2,1)S(1)} %get-tuple-element.148) | copy-start | bytes 373252
  168.1 9.4 %copy-start.72 = (bf16[6,7,7,256]{3,2,1,0:T(8,128)(2,1)}, bf16[6,7,7,256]{3,2,1,0:T(8,128)(2,1)S(1)}, u32[]{:S(2)}) copy-start(bf16[6,7,7,256]{3,2,1,0:T(8,128)(2,1)S(1)} %get-tuple-element.192) | copy-start | bytes 451588
  168.1 10.1 %copy-start.70 = (bf16[6,7,7,256]{3,2,1,0:T(8,128)(2,1)}, bf16[6,7,7,256]{3,2,1,0:T(8,128)(2,1)S(1)}, u32[]{:S(2)}) copy-start(bf16[6,7,7,256]{3,2,1,0:T(8,128)(2,1)S(1)} %get-tuple-element.193) | copy-start | bytes 451588
  168.1 10.9 %copy-start.68 = (bf16[6,7,7,256]{3,2,1,0:T(8,128)(2,1)}, bf16[6,7,7,256]{3,2,1,0:T(8,128)(2,1)S(1)}, u32[]{:S(2)}) copy-start(bf16[6,7,7,256]{3,2,1,0:T(8,128)(2,1)S(1)} %get-tuple-element.194) | copy-start | bytes 451588
  168.2 11.6 %copy-start.66 = (bf16[6,7,7,256]{3,2,1,0:T(8,128)(2,1)}, bf16[6,7,7,256]{3,2,1,0:T(8,128)(2,1)S(1)}, u32[]{:S(2)}) copy-start(bf16[6,7,7,256]{3,2,1,0:T(8,128)(2,1)S(1)} %get-tuple-element.188) | copy-start | bytes 451588
  184.5 9.7 %copy-start.47 = (bf16[3,9,9,256]{3,2,1,0:T(8,128)(2,1)}, bf16[3,9,9,256]{3,2,1,0:T(8,128)(2,1)S(1)}, u32[]{:S(2)}) copy-start(bf16[3,9,9,256]{3,2,1,0:T(8,128)(2,1)S(1)} %get-tuple-element.161) | copy-start | bytes 373252
  184.5 10.4 %copy-start.45 = (bf16[3,9,9,256]{3,2,1,0:T(8,128)(2,1)}, bf16[3,9,9,256]{3,2,1,0:T(8,128)(2,1)S(1)}, u32[]{:S(2)}) copy-start(bf16[3,9,9,256]{3,2,1,0:T(8,128)(2,1)S(1)} %get-tuple-element.162) | copy-start | bytes 373252
  184.5 11.1 %copy-start.43 = (bf16[3,9,9,256]{3,2,1,0:T(8,128)(2,1)}, bf16[3,9,9,256]{3,2,1,0:T(8,128)(2,1)S(1)}, u32[]{:S(2)}) copy-start(bf16[3,9,9,256]{3,2,1,0:T(8,128)(2,1)S(1)} %get-tuple-element.156) | copy-start | bytes 373252
  197.2 26.2 %copy-start.22 = (f32[150,256]{1,0:T(8,128)}, f32[150,256]{1,0:T(8,128)S(1)}, u32[]{:S(2)}) copy-start(f32[150,256]{1,0:T(8,128)S(1)} %convolution_add_fusion.92) | copy-start | bytes 460804
  198.6 24.8 %copy-start.6 = (f32[294,256]{1,0:T(8,128)}, f32[294,256]{1,0:T(8,128)S(1)}, u32[]{:S(2)}) copy-start(f32[294,256]{1,0:T(8,128)S(1)} %convolution_add_fusion.28) | copy-start | bytes 903172
  200.9 22.5 %copy-start.24 = (f32[150,256]{1,0:T(8,128)}, f32[150,256]{1,0:T(8,128)S(1)}, u32[]{:S(2)}) copy-start(f32[150,256]{1,0:T(8,128)S(1)} %convolution_add_fusion.84) | copy-start | bytes 460804
  202.2 21.2 %copy-start.8 = (f32[294,256]{1,0:T(8,128)}, f32[294,256]{1,0:T(8,128)S(1)}, u32[]{:S(2)}) copy-start(f32[294,256]{1,0:T(8,128)S(1)} %convolution_add_fusion.20) | copy-start | bytes 903172
  203.2 18.2 %copy-start.294 = (f32[256]{0:T(256)S(1)}, f32[256]{0:T(256)}, u32[]{:S(2)}) copy-start(f32[256]{0:T(256)} %param.27) | copy-start | bytes 3076
  203.2 20.2 %copy-start.310 = (f32[256]{0:T(256)S(1)}, f32[256]{0:T(256)}, u32[]{:S(2)}) copy-start(f32[256]{0:T(256)} %param.28) | copy-start | bytes 3076
  203.4 21.5 %copy-start.10 = (f32[243,256]{1,0:T(8,128)}, f32[243,256]{1,0:T(8,128)S(1)}, u32[]{:S(2)}) copy-start(f32[243,256]{1,0:T(8,128)S(1)} %convolution_add_fusion.52) | copy-start | bytes 746500
  225.0 44.7 %all-gather.15.cloned.1.call-start = ((), (), s32[]{:S(2)}) async-start(), calls=%async_computation.5 | async-start | bytes 1761280 | tf_op jit(solution)/shard_map/all_gather | solution.py:177
  227.8 24.4 %all-to-all-start = ((bf16[256,4,512]{0,2,1:T(8,128)(2,1)}), bf16[256,4,512]{0,2,1:T(8,128)(2,1)S(1)}, u32[]{:S(2)}, u32[]{:S(2)}) async-start(bf16[256,4,512]{0,2,1:T(8,128)(2,1)} %bitcast.592), calls=%async_computation | async-start | bytes 2097152 | tf_op jit(solution)/shard_map/all_to_all | solution.py:131
  231.3 158.1 %all-gather.21.cloned.1.call-start = ((), (), s32[]{:S(2)}) async-start(), calls=%async_computation.8 | async-start | bytes 3522560 | tf_op jit(solution)/shard_map/all_gather | solution.py:206
  253.5 16.1 %copy-start.153 = (bf16[4,256,512]{2,1,0:T(8,128)(2,1)S(1)}, bf16[4,256,512]{2,1,0:T(8,128)(2,1)}, u32[]{:S(2)}) copy-start(bf16[4,256,512]{2,1,0:T(8,128)(2,1)} %copy.220) | copy-start | bytes 3145732
  257.3 37.3 %copy-start.293 = (f32[512]{0:T(512)S(1)}, f32[512]{0:T(512)}, u32[]{:S(2)}) copy-start(f32[512]{0:T(512)} %param.29) | copy-start | bytes 6148
  296.6 9.4 %copy-start.269 = (f32[512]{0:T(512)}, f32[512]{0:T(512)S(1)}, u32[]{:S(2)}) copy-start(f32[512]{0:T(512)S(1)} %get-tuple-element.238) | copy-start | bytes 6148
  306.0 21.4 %copy-start.3 = (f32[687,512]{1,0:T(8,128)}, f32[687,512]{1,0:T(8,128)S(1)}, u32[]{:S(2)}) copy-start(f32[687,512]{1,0:T(8,128)S(1)} %get-tuple-element.231) | copy-start | bytes 4220932
  327.4 66.2 %all-gather.17.cloned.1.call-start = ((), (), s32[]{:S(2)}) async-start(), calls=%async_computation.6 | async-start | bytes 3522560 | tf_op jit(solution)/shard_map/all_gather | solution.py:206
  331.2 293.3 %all-gather.19.cloned.1.call-start = ((), (), s32[]{:S(2)}) async-start(), calls=%async_computation.7 | async-start | bytes 1761280 | tf_op jit(solution)/shard_map/all_gather | solution.py:251
  393.7 23.8 %copy-start.307 = (f32[256]{0:T(256)S(1)}, f32[256]{0:T(256)}, u32[]{:S(2)}) copy-start(f32[256]{0:T(256)} %get-tuple-element.117) | copy-start | bytes 3076
  529.7 18.2 %copy-start.297 = (f32[256]{0:T(256)S(1)}, f32[256]{0:T(256)}, u32[]{:S(2)}) copy-start(f32[256]{0:T(256)} %get-tuple-element.110) | copy-start | bytes 3076
  530.7 19.5 %copy-start.163 = (bf16[294,256]{0,1:T(8,128)(2,1)S(1)}, bf16[294,256]{0,1:T(8,128)(2,1)}, u32[]{:S(2)}) copy-start(bf16[294,256]{0,1:T(8,128)(2,1)} %copy.234) | copy-start | bytes 451588
  549.6 78.6 %all-gather.23.cloned.1.call-start = ((), (), s32[]{:S(2)}) async-start(), calls=%async_computation.9 | async-start | bytes 1761280 | tf_op jit(solution)/shard_map/all_gather | solution.py:251
  580.4 210.5 %all-reduce.21.cloned.1.call-start = ((), (), s32[]{:S(2)}) async-start(), calls=%async_computation.10 | async-start | bytes 10747904 | tf_op jit(solution)/shard_map/psum | solution.py:264
  (277 other events, 793.7 us)
Sparse Core Ops, SparseCore 0:
  16.2 29.3 all-gather.8
  47.7 26.6 all-gather.12
  225.0 22.2 all-gather.10
  248.8 20.8 all-gather.14
  327.6 24.4 all-gather.20
  354.0 26.6 all-gather.16
  549.8 16.7 all-gather.18
  580.5 16.7 all-gather.22
  602.5 188.4 all-reduce.20
where the time goes:
time: 817 us; the launch traced here: 804 us
  local copies, waits for them, and re-layouts  274 us (34%)
  waiting for transfers between devices  198 us (24%)
  blocking collectives  133 us (16%)
  matrix products  122 us (15%)
  other arithmetic  50.3 us (6%)
  between operations  21.4 us (3%)
    psum x1, waiting for transfers between devices, per_device(): lax.psum((reduce_acc, group_acc, expand_acc), 'batch')  150 us
    reshape x96, local copies, waits for them, and re-layouts, tap_conv(): window = padded[:, row_start:row_start + edge_size, col_start:col_start +...  104 us
    dot_general x108, matrix products, tap_conv(): jnp.dot(window, matrices[tap_index], preferred_element_type=jnp.float32)  63.5 us
    reshape x48, local copies, waits for them, and re-layouts, kernel_grad(): window = padded[:, row_start:row_start + edge_size, col_start:col_start +...  52.8 us
    all_gather x2, waiting for transfers between devices, per_device(): full_maps = lax.all_gather(local_maps, 'tensor', axis=1, tiled=True)  35.8 us
    unnamed x635, local copies, waits for them, and re-layouts  32.4 us
    dot_general x54, matrix products, kernel_grad(): jnp.einsum('pgi,pgo->gio', window, grad_part, preferred_element_type=jnp....  23.1 us
    slice x12, local copies, waits for them, and re-layouts, tap_conv(): padded[:, row_start:row_start + edge_size, col_start:col_start + edge_siz...  23.1 us
  transfers between devices with their start and end apart: 10, of which 4 were waited for; matrix products, arithmetic and copies ran while one was open for 22% of the time, Pallas kernels for 0%

commit v1 on v0

--- a/solution.py
+++ b/solution.py
@@ -4,6 +4,12 @@
 from jax.sharding import PartitionSpec as P
 
 EPSILON = 1e-05
+
+
+def laid_out(tiles, dim):
+    dims = list(tiles.shape[1:])
+    dims[dim] *= tiles.shape[0]
+    return jnp.moveaxis(tiles, 0, dim).reshape(dims)
 
 
 def slope(values):
@@ -157,7 +163,19 @@
                 counts_now[column] * edges[column] * edges[column]
             ).astype(jnp.float32)
         live_mask = jnp.concatenate(mask_pieces, 0)[:, None]
-        full_maps = lax.all_gather(local_maps, "tensor", axis=1, tiled=True)
+        size = lax.axis_size("tensor")
+        pairs = [(i, (i + 1) % size) for i in range(size)]
+        back = [(b, a) for a, b in pairs]
+        lower, upper = ([], [])
+        for step in range(size - 1):
+            if step % 2 == 0:
+                lower.append(lax.ppermute(lower[-1] if lower else local_maps, "tensor", pairs))
+            else:
+                upper.append(lax.ppermute(upper[-1] if upper else local_maps, "tensor", back))
+        parts = jnp.stack([*lower[::-1], local_maps, *upper])
+        shift = lax.axis_index("tensor") - len(lower)
+        parts = parts[(jnp.arange(size) - shift) % size]
+        full_maps = laid_out(parts, 1)
         first = jnp.dot(full_maps, reduce_weight, preferred_element_type=jnp.float32)
         sum_one, square_one, pixel_total = lax.psum(
             (jnp.sum(live_mask * first, 0), jnp.sum(live_mask * first * first, 0), local_pixels),

time: 817 us -> 833 us (1.020)
  local copies, waits for them, and re-layouts: 274 us -> 306 us
  waiting for transfers between devices: 198 us -> 177 us
  starting transfers between devices: 4.7 us -> 14.1 us
    all_gather x2 -> x0, waiting for transfers between devices: 35.8 us -> none  [per_device(): full_maps = lax.all_gather(local_maps, 'tensor', axis=1, tiled=True)]
    ppermute x0 -> x6, waiting for transfers between devices: none -> 13 us  [the longest x4 13 us: per_device(): lax.ppermute(lower[-1] if lower else local_maps, 'tensor', pairs)]
    ppermute x0 -> x6, starting transfers between devices: none -> 9.32 us  [the longest x4 6.19 us: per_device(): lax.ppermute(lower[-1] if lower else local_maps, 'tensor', pairs)]
    unnamed x635 -> x625, local copies, waits for them, and re-layouts: 32.4 us -> 40.1 us
  transfers between devices with their start and end apart: 10 -> 14, of which waited for: 4 -> 5; matrix products, arithmetic and copies ran while one was open for 22% -> 22% of each run, Pallas kernels for 0% -> 0%
where the time goes in v1:
time: 833 us; the launch traced here: 822 us
  local copies, waits for them, and re-layouts  306 us (37%)
  waiting for transfers between devices  177 us (21%)
  blocking collectives  134 us (16%)
  matrix products  115 us (14%)
  other arithmetic  54.8 us (7%)
  between operations  21.6 us (3%)
  starting transfers between devices  14.1 us (2%)
    psum x1, waiting for transfers between devices, per_device(): lax.psum((reduce_acc, group_acc, expand_acc), 'batch')  152 us
    reshape x96, local copies, waits for them, and re-layouts, tap_conv(): window = padded[:, row_start:row_start + edge_size, col_start:col_start +...  106 us
    dot_general x108, matrix products, tap_conv(): jnp.dot(window, matrices[tap_index], preferred_element_type=jnp.float32)  66.9 us
    reshape x48, local copies, waits for them, and re-layouts, kernel_grad(): window = padded[:, row_start:row_start + edge_size, col_start:col_start +...  53.6 us
    unnamed x625, local copies, waits for them, and re-layouts  40.1 us
    psum x1, blocking collectives, per_device(): lax.psum((jnp.sum(live_mask * first, 0), jnp.sum(live_mask * first * firs...  23.6 us
    slice x12, local copies, waits for them, and re-layouts, tap_conv(): padded[:, row_start:row_start + edge_size, col_start:col_start + edge_siz...  23 us
    psum x1, blocking collectives, per_device(): lax.psum((jnp.sum(live_mask * third, 0), jnp.sum(live_mask * third * thir...  22.2 us
  transfers between devices with their start and end apart: 14, of which 5 were waited for; matrix products, arithmetic and copies ran while one was open for 22% of the time, Pallas kernels for 0%

profile of v1, /device:TPU:0, one launch (start us, length us, event | category | flops | bytes accessed | tf_op | source)
XLA Modules:
  0.0 821.9 jit_solution(18258117424413531034)
XLA Ops:
  7.2 3.5 slice_reduce_fusion.7
  11.0 2.6 slice_reduce_fusion.3
  28.5 3.4 collective-permute-done.3
  31.9 2.4 collective-permute-start.4
  34.3 3.9 multiply_bitcast_fusion
  38.2 8.7 %collective-permute-done = bf16[687,512]{1,0:T(8,128)(2,1)S(1)} collective-permute-done((bf16[687,512]{1,0:T(8,128)(2,1)S(1)}, bf16[687,512]{1,0:T(8,128)(2,1)S(1)}, u32[]{:S(2)}, u32[]{:S(2)}) %collective-permute-start) | collective-permute-done | bytes 703520 | tf_op jit(solution)/shard_map/ppermute | solution.py:172
  46.9 2.7 collective-permute-start.1
  50.4 5.8 reshape.721
  57.2 3.1 pad_maximum_fusion.1
  60.3 4.1 gather_fusion.1
  64.5 4.0 copy.224
  69.5 2.5 copy.306
  72.0 3.1 pad_maximum_fusion
  75.1 4.1 gather_fusion
  79.2 4.0 copy.221
  88.8 23.6 %all-reduce.17 = (f32[256]{0:T(256)S(1)}, f32[]{:T(128)}, f32[256]{0:T(256)S(1)}, f32[256]{0:T(256)S(1)}, f32[]{:T(128)}, /*index=5*/f32[256]{0:T(256)S(1)}) all-reduce(f32[256]{0:T(256)S(1)} %get-tuple-element.60, f32[]{:T(128)S(6)} %add.665, f32[256]{0:T(256)S(1)} %get-tuple-element.59, ...), channel_id=1, replica_groups=mesh['batch'=8,'tensor'=4] {'batch'}, use_global_device_ids=true, to_apply=%region_14.15 | all-reduce | flops 1026 | bytes 8208 | tf_op jit(solution)/shard_map/psum | solution.py:180
  118.2 2.5 pad_slice_fusion.88
  133.1 3.0 pad_slice_fusion.24
  152.8 3.3 pad_slice_fusion.56
  183.5 2.9 pad_slice_fusion.16
  200.3 3.3 pad_slice_fusion.48
  225.3 17.3 %all-reduce.16 = (f32[256]{0:T(256)S(1)}, f32[256]{0:T(256)S(1)}, f32[256]{0:T(256)S(1)}, f32[256]{0:T(256)S(1)}) all-reduce(f32[256]{0:T(256)S(1)} %get-tuple-element.56, f32[256]{0:T(256)S(1)} %get-tuple-element.55, f32[256]{0:T(256)S(1)} %get-tuple-element.54, ...), channel_id=1, replica_groups=mesh['batch'=8,'tensor'=4] {'batch'}, use_global_device_ids=true, to_apply=%region_19.20 | all-reduce | flops 1024 | bytes 8192 | tf_op jit(solution)/shard_map/psum | solution.py:188
  248.9 3.5 all-to-all-start
  252.5 4.3 slice_reduce_fusion.5
  260.5 4.8 slice_reduce_fusion.1
  268.9 3.2 slice_reduce_fusion.9
  276.8 3.6 multiply_reduce_fusion.1
  280.5 11.2 %all-gather.9.cloned.1.call-done = bf16[687,1024]{1,0:T(8,128)(2,1)} async-done(((bf16[687,256]{1,0:T(8,128)(2,1)}), bf16[687,1024]{1,0:T(8,128)(2,1)}) %all-gather.9.cloned.1.call-update) | async-done | bytes 1406992 | tf_op jit(solution)/shard_map/all_gather | solution.py:195
  291.7 3.6 multiply_reduce_fusion
  295.3 22.2 %all-reduce.15 = (f32[512]{0:T(512)}, f32[512]{0:T(512)}, f32[512]{0:T(512)}, f32[512]{0:T(512)}) all-reduce(f32[512]{0:T(512)S(1)} %get-tuple-element.48, f32[512]{0:T(512)S(1)} %get-tuple-element.47, f32[512]{0:T(512)S(1)} %get-tuple-element.46, f32[512]{0:T(512)S(1)} %get-tuple-element.45), channel_id=1, replica_groups=mesh['batch'=8,'tensor'=4] {'batch'}, use_global_device_ids=true, to_apply=%region_25.26 | all-reduce | flops 2048 | bytes 16384 | tf_op jit(solution)/shard_map/psum | solution.py:199
  317.5 2.5 fusion.151
  320.0 7.5 fusion.139
  327.5 17.5 %all-reduce.14 = (f32[512]{0:T(512)S(1)}, f32[512]{0:T(512)S(1)}, f32[512]{0:T(512)S(1)}, f32[512]{0:T(512)S(1)}) all-reduce(f32[512]{0:T(512)} %get-tuple-element.229, f32[512]{0:T(512)} %get-tuple-element.230, f32[512]{0:T(512)} %get-tuple-element.50, f32[512]{0:T(512)} %get-tuple-element.49), channel_id=1, replica_groups=mesh['batch'=8,'tensor'=4] {'batch'}, use_global_device_ids=true, to_apply=%region_41.42 | all-reduce | flops 2048 | bytes 16384 | tf_op jit(solution)/shard_map/psum | solution.py:209
  345.1 3.6 multiply_convert_fusion
  348.8 3.7 multiply_convert_fusion.1
  413.3 4.2 fusion.144
  417.5 4.1 fusion.142
  421.6 19.1 %all-reduce.13 = (f32[256]{0:T(256)S(1)}, f32[256]{0:T(256)S(1)}, f32[256]{0:T(256)S(1)}, f32[256]{0:T(256)S(1)}) all-reduce(f32[256]{0:T(256)S(1)} %get-tuple-element.68, f32[256]{0:T(256)S(1)} %get-tuple-element.67, f32[256]{0:T(256)S(1)} %get-tuple-element.64, ...), channel_id=1, replica_groups=mesh['batch'=8,'tensor'=4] {'batch'}, use_global_device_ids=true, to_apply=%region_45.46 | all-reduce | flops 1024 | bytes 8192 | tf_op jit(solution)/shard_map/psum | solution.py:232
  552.9 17.3 %all-reduce.12 = (f32[256]{0:T(256)S(1)}, f32[256]{0:T(256)S(1)}, f32[256]{0:T(256)S(1)}, f32[256]{0:T(256)S(1)}) all-reduce(f32[256]{0:T(256)S(1)} %get-tuple-element.232, f32[256]{0:T(256)S(1)} %get-tuple-element.233, f32[256]{0:T(256)S(1)} %get-tuple-element.62, ...), channel_id=1, replica_groups=mesh['batch'=8,'tensor'=4] {'batch'}, use_global_device_ids=true, to_apply=%region_49.50 | all-reduce | flops 1024 | bytes 8192 | tf_op jit(solution)/shard_map/psum | solution.py:250
  570.1 2.7 multiply_convert_fusion.6
  599.1 3.0 fusion.154
  604.3 2.3 convolution_add_fusion
  606.7 2.4 convolution_add_fusion.1
  613.6 16.9 %all_to_all.38 = bf16[4,512,256]{2,1,0:T(8,128)(2,1)S(1)} all-to-all(bf16[4,512,256]{2,1,0:T(8,128)(2,1)S(1)} %bitcast.622), channel_id=1, replica_groups=mesh['batch'=8,'tensor'=4] {'tensor'}, dimensions={0} | all-to-all | bytes 2097152 | tf_op jit(solution)/shard_map/all_to_all | solution.py:138
  641.2 2.5 convolution_add_fusion.3
  645.7 2.5 convolution_add_fusion.2
  656.6 151.7 %all-reduce.21.cloned.1.call-done = (f32[2048,256]{1,0:T(8,128)}, f32[3,3,8,32,32]{4,3,2,1,0:T(8,128)}, f32[256,2048]{1,0:T(8,128)}) async-done(((f32[2048,256]{1,0:T(8,128)}, f32[3,3,8,32,32]{4,3,2,1,0:T(8,128)}, f32[256,2048]{1,0:T(8,128)}), (f32[2048,256]{1,0:T(8,128)}, f32[3,3,8,32,32]{4,3,2,1,0:T(8,128)}, f32[256,2048]{1,0:T(8,128)})) %all-reduce.21.cloned.1.call-update) | async-done | bytes 4489232 | tf_op jit(solution)/shard_map/psum | solution.py:282
  808.4 3.1 copy.454
  (1092 shorter events, 363.4 us)
Async XLA Ops:
  7.2 269.6 %all-gather.7.cloned.1.call-start = ((), (), s32[]{:S(2)}) async-start(), calls=%async_computation.2 | async-start | bytes 1761280 | tf_op jit(solution)/shard_map/all_gather | solution.py:195
  15.6 41.6 %copy-start.6 = (bf16[687,512]{1,0:T(8,128)(2,1)}, bf16[687,512]{1,0:T(8,128)(2,1)S(1)}, u32[]{:S(2)}) copy-start(bf16[687,512]{1,0:T(8,128)(2,1)S(1)} %get-tuple-element.264) | copy-start | bytes 2110468
  15.7 56.4 %copy-start.4 = (bf16[687,512]{1,0:T(8,128)(2,1)}, bf16[687,512]{1,0:T(8,128)(2,1)S(1)}, u32[]{:S(2)}) copy-start(bf16[687,512]{1,0:T(8,128)(2,1)S(1)} %get-tuple-element.263) | copy-start | bytes 2110468
  15.7 16.2 %collective-permute-start.3 = (bf16[687,512]{1,0:T(8,128)(2,1)S(1)}, bf16[687,512]{1,0:T(8,128)(2,1)}, u32[]{:S(2)}, u32[]{:S(2)}) collective-permute-start(bf16[687,512]{1,0:T(8,128)(2,1)S(1)} %get-tuple-element.264), channel_id=1, source_target_pairs={{0,1},{1,2},{2,3},{3,0},{4,5},{5,6},{6,7},{7,4},{8,9},{9,10},{10,1... | collective-permute-start | bytes 2110472 | tf_op jit(solution)/shard_map/ppermute | solution.py:172
  16.2 40.1 %collective-permute-start.5 = (bf16[687,512]{1,0:T(8,128)(2,1)S(1)}, bf16[687,512]{1,0:T(8,128)(2,1)}, u32[]{:S(2)}, u32[]{:S(2)}) collective-permute-start(bf16[687,512]{1,0:T(8,128)(2,1)S(1)} %get-tuple-element.264), channel_id=1, source_target_pairs={{1,0},{2,1},{3,2},{0,3},{5,4},{6,5},{7,6},{4,7},{9,8},{10,9},{11,1... | collective-permute-start | bytes 2110472 | tf_op jit(solution)/shard_map/ppermute | solution.py:174
  18.2 28.7 %collective-permute-start = (bf16[687,512]{1,0:T(8,128)(2,1)S(1)}, bf16[687,512]{1,0:T(8,128)(2,1)S(1)}, u32[]{:S(2)}, u32[]{:S(2)}) collective-permute-start(bf16[687,512]{1,0:T(8,128)(2,1)S(1)} %get-tuple-element.263), channel_id=1, source_target_pairs={{0,1},{1,2},{2,3},{3,0},{4,5},{5,6},{6,7},{7,4},{8,9},{9,10},{10,1... | collective-permute-start | bytes 2110472 | tf_op jit(solution)/shard_map/ppermute | solution.py:172
  18.8 53.2 %collective-permute-start.2 = (bf16[687,512]{1,0:T(8,128)(2,1)S(1)}, bf16[687,512]{1,0:T(8,128)(2,1)}, u32[]{:S(2)}, u32[]{:S(2)}) collective-permute-start(bf16[687,512]{1,0:T(8,128)(2,1)S(1)} %get-tuple-element.263), channel_id=1, source_target_pairs={{1,0},{2,1},{3,2},{0,3},{5,4},{6,5},{7,6},{4,7},{9,8},{10,9},{11,1... | collective-permute-start | bytes 2110472 | tf_op jit(solution)/shard_map/ppermute | solution.py:174
  31.9 25.3 %collective-permute-start.4 = (bf16[687,512]{1,0:T(8,128)(2,1)}, bf16[687,512]{1,0:T(8,128)(2,1)}, u32[]{:S(2)}, u32[]{:S(2)}) collective-permute-start(bf16[687,512]{1,0:T(8,128)(2,1)} %collective-permute-done.3), channel_id=1, source_target_pairs={{0,1},{1,2},{2,3},{3,0},{4,5},{5,6},{6,7},{7,4},{8,9},{9,10},{10,1... | collective-permute-start | bytes 2110472 | tf_op jit(solution)/shard_map/ppermute | solution.py:172
  46.9 25.1 %collective-permute-start.1 = (bf16[687,512]{1,0:T(8,128)(2,1)S(1)}, bf16[687,512]{1,0:T(8,128)(2,1)}, u32[]{:S(2)}, u32[]{:S(2)}) collective-permute-start(bf16[687,512]{1,0:T(8,128)(2,1)S(1)} %collective-permute-done), channel_id=1, source_target_pairs={{0,1},{1,2},{2,3},{3,0},{4,5},{5,6},{6,7},{7,4},{8,9},{9,10},{10,1... | collective-permute-start | bytes 2110472 | tf_op jit(solution)/shard_map/ppermute | solution.py:172
  87.8 24.6 %copy-start.277 = (f32[256]{0:T(256)S(1)}, f32[256]{0:T(256)}, u32[]{:S(2)}) copy-start(f32[256]{0:T(256)} %param.25) | copy-start | bytes 3076
  87.8 26.4 %copy-start.302 = (f32[256]{0:T(256)S(1)}, f32[256]{0:T(256)}, u32[]{:S(2)}) copy-start(f32[256]{0:T(256)} %param.26) | copy-start | bytes 3076
  88.7 26.7 %copy-start.2 = (f32[687,256]{1,0:T(8,128)}, f32[687,256]{1,0:T(8,128)S(1)}, u32[]{:S(2)}) copy-start(f32[687,256]{1,0:T(8,128)S(1)} %get-tuple-element.256) | copy-start | bytes 2110468
  117.5 82.1 %copy-start.115 = (bf16[243,256]{1,0:T(8,128)(2,1)}, bf16[243,256]{1,0:T(8,128)(2,1)S(1)}, u32[]{:S(2)}) copy-start(bf16[243,256]{1,0:T(8,128)(2,1)S(1)} %slice.831) | copy-start | bytes 373252
  120.7 11.0 %copy-start.119 = (bf16[6,5,5,256]{3,2,1,0:T(8,128)(2,1)}, bf16[6,5,5,256]{3,2,1,0:T(8,128)(2,1)S(1)}, u32[]{:S(2)}) copy-start(bf16[6,5,5,256]{3,2,1,0:T(8,128)(2,1)S(1)} %get-tuple-element.212) | copy-start | bytes 230404
  136.1 12.1 %copy-start.57 = (bf16[6,7,7,256]{3,2,1,0:T(8,128)(2,1)}, bf16[6,7,7,256]{3,2,1,0:T(8,128)(2,1)S(1)}, u32[]{:S(2)}) copy-start(bf16[6,7,7,256]{3,2,1,0:T(8,128)(2,1)S(1)} %get-tuple-element.184) | copy-start | bytes 451588
  136.1 12.8 %copy-start.55 = (bf16[6,7,7,256]{3,2,1,0:T(8,128)(2,1)}, bf16[6,7,7,256]{3,2,1,0:T(8,128)(2,1)S(1)}, u32[]{:S(2)}) copy-start(bf16[6,7,7,256]{3,2,1,0:T(8,128)(2,1)S(1)} %get-tuple-element.185) | copy-start | bytes 451588
  136.1 13.6 %copy-start.53 = (bf16[6,7,7,256]{3,2,1,0:T(8,128)(2,1)}, bf16[6,7,7,256]{3,2,1,0:T(8,128)(2,1)S(1)}, u32[]{:S(2)}) copy-start(bf16[6,7,7,256]{3,2,1,0:T(8,128)(2,1)S(1)} %get-tuple-element.186) | copy-start | bytes 451588
  136.1 14.3 %copy-start.51 = (bf16[6,7,7,256]{3,2,1,0:T(8,128)(2,1)}, bf16[6,7,7,256]{3,2,1,0:T(8,128)(2,1)S(1)}, u32[]{:S(2)}) copy-start(bf16[6,7,7,256]{3,2,1,0:T(8,128)(2,1)S(1)} %get-tuple-element.180) | copy-start | bytes 451588
  156.0 13.8 %copy-start.33 = (bf16[3,9,9,256]{3,2,1,0:T(8,128)(2,1)}, bf16[3,9,9,256]{3,2,1,0:T(8,128)(2,1)S(1)}, u32[]{:S(2)}) copy-start(bf16[3,9,9,256]{3,2,1,0:T(8,128)(2,1)S(1)} %get-tuple-element.153) | copy-start | bytes 373252
  156.0 14.5 %copy-start.31 = (bf16[3,9,9,256]{3,2,1,0:T(8,128)(2,1)}, bf16[3,9,9,256]{3,2,1,0:T(8,128)(2,1)S(1)}, u32[]{:S(2)}) copy-start(bf16[3,9,9,256]{3,2,1,0:T(8,128)(2,1)S(1)} %get-tuple-element.154) | copy-start | bytes 373252
  156.0 15.2 %copy-start.29 = (bf16[3,9,9,256]{3,2,1,0:T(8,128)(2,1)}, bf16[3,9,9,256]{3,2,1,0:T(8,128)(2,1)S(1)}, u32[]{:S(2)}) copy-start(bf16[3,9,9,256]{3,2,1,0:T(8,128)(2,1)S(1)} %get-tuple-element.148) | copy-start | bytes 373252
  186.4 11.0 %copy-start.65 = (bf16[6,7,7,256]{3,2,1,0:T(8,128)(2,1)}, bf16[6,7,7,256]{3,2,1,0:T(8,128)(2,1)S(1)}, u32[]{:S(2)}) copy-start(bf16[6,7,7,256]{3,2,1,0:T(8,128)(2,1)S(1)} %get-tuple-element.193) | copy-start | bytes 451588
  186.4 11.8 %copy-start.63 = (bf16[6,7,7,256]{3,2,1,0:T(8,128)(2,1)}, bf16[6,7,7,256]{3,2,1,0:T(8,128)(2,1)S(1)}, u32[]{:S(2)}) copy-start(bf16[6,7,7,256]{3,2,1,0:T(8,128)(2,1)S(1)} %get-tuple-element.194) | copy-start | bytes 451588
  186.4 12.5 %copy-start.61 = (bf16[6,7,7,256]{3,2,1,0:T(8,128)(2,1)}, bf16[6,7,7,256]{3,2,1,0:T(8,128)(2,1)S(1)}, u32[]{:S(2)}) copy-start(bf16[6,7,7,256]{3,2,1,0:T(8,128)(2,1)S(1)} %get-tuple-element.188) | copy-start | bytes 451588
  203.7 11.2 %copy-start.44 = (bf16[3,9,9,256]{3,2,1,0:T(8,128)(2,1)}, bf16[3,9,9,256]{3,2,1,0:T(8,128)(2,1)S(1)}, u32[]{:S(2)}) copy-start(bf16[3,9,9,256]{3,2,1,0:T(8,128)(2,1)S(1)} %get-tuple-element.160) | copy-start | bytes 373252
  203.7 11.9 %copy-start.43 = (bf16[3,9,9,256]{3,2,1,0:T(8,128)(2,1)}, bf16[3,9,9,256]{3,2,1,0:T(8,128)(2,1)S(1)}, u32[]{:S(2)}) copy-start(bf16[3,9,9,256]{3,2,1,0:T(8,128)(2,1)S(1)} %get-tuple-element.161) | copy-start | bytes 373252
  203.7 12.6 %copy-start.42 = (bf16[3,9,9,256]{3,2,1,0:T(8,128)(2,1)}, bf16[3,9,9,256]{3,2,1,0:T(8,128)(2,1)S(1)}, u32[]{:S(2)}) copy-start(bf16[3,9,9,256]{3,2,1,0:T(8,128)(2,1)S(1)} %get-tuple-element.162) | copy-start | bytes 373252
  203.7 13.3 %copy-start.40 = (bf16[3,9,9,256]{3,2,1,0:T(8,128)(2,1)}, bf16[3,9,9,256]{3,2,1,0:T(8,128)(2,1)S(1)}, u32[]{:S(2)}) copy-start(bf16[3,9,9,256]{3,2,1,0:T(8,128)(2,1)S(1)} %get-tuple-element.156) | copy-start | bytes 373252
  221.2 23.2 %copy-start.11 = (f32[243,256]{1,0:T(8,128)}, f32[243,256]{1,0:T(8,128)S(1)}, u32[]{:S(2)}) copy-start(f32[243,256]{1,0:T(8,128)S(1)} %convolution_add_fusion.60) | copy-start | bytes 746500
  222.3 22.1 %copy-start.25 = (f32[150,256]{1,0:T(8,128)}, f32[150,256]{1,0:T(8,128)S(1)}, u32[]{:S(2)}) copy-start(f32[150,256]{1,0:T(8,128)S(1)} %convolution_add_fusion.84) | copy-start | bytes 460804
  223.6 20.8 %copy-start.9 = (f32[294,256]{1,0:T(8,128)}, f32[294,256]{1,0:T(8,128)S(1)}, u32[]{:S(2)}) copy-start(f32[294,256]{1,0:T(8,128)S(1)} %convolution_add_fusion.20) | copy-start | bytes 903172
  224.7 18.0 %copy-start.289 = (f32[256]{0:T(256)S(1)}, f32[256]{0:T(256)}, u32[]{:S(2)}) copy-start(f32[256]{0:T(256)} %param.27) | copy-start | bytes 3076
  224.7 19.7 %copy-start.304 = (f32[256]{0:T(256)S(1)}, f32[256]{0:T(256)}, u32[]{:S(2)}) copy-start(f32[256]{0:T(256)} %param.28) | copy-start | bytes 3076
  224.9 21.0 %copy-start.13 = (f32[243,256]{1,0:T(8,128)}, f32[243,256]{1,0:T(8,128)S(1)}, u32[]{:S(2)}) copy-start(f32[243,256]{1,0:T(8,128)S(1)} %convolution_add_fusion.52) | copy-start | bytes 746500
  245.9 45.8 %all-gather.9.cloned.1.call-start = ((), (), s32[]{:S(2)}) async-start(), calls=%async_computation.3 | async-start | bytes 1761280 | tf_op jit(solution)/shard_map/all_gather | solution.py:195
  248.9 26.6 %all-to-all-start = ((bf16[256,4,512]{0,2,1:T(8,128)(2,1)}), bf16[256,4,512]{0,2,1:T(8,128)(2,1)S(1)}, u32[]{:S(2)}, u32[]{:S(2)}) async-start(bf16[256,4,512]{0,2,1:T(8,128)(2,1)} %bitcast.618), calls=%async_computation | async-start | bytes 2097152 | tf_op jit(solution)/shard_map/all_to_all | solution.py:137
  252.5 160.8 %all-gather.15.cloned.1.call-start = ((), (), s32[]{:S(2)}) async-start(), calls=%async_computation.6 | async-start | bytes 3522560 | tf_op jit(solution)/shard_map/all_gather | solution.py:224
  280.5 37.0 %copy-start.288 = (f32[512]{0:T(512)S(1)}, f32[512]{0:T(512)}, u32[]{:S(2)}) copy-start(f32[512]{0:T(512)} %param.29) | copy-start | bytes 6148
  280.5 39.5 %copy-start.5 = (bf16[687,512]{1,0:T(8,128)(2,1)S(1)}, bf16[687,512]{1,0:T(8,128)(2,1)}, u32[]{:S(2)}) copy-start(bf16[687,512]{1,0:T(8,128)(2,1)} %copy-done.4) | copy-start | bytes 2110468
  280.5 39.5 %copy-start.101 = (bf16[294,512]{1,0:T(8,128)(2,1)S(1)}, bf16[294,512]{1,0:T(8,128)(2,1)}, u32[]{:S(2)}) copy-start(bf16[294,512]{1,0:T(8,128)(2,1)} %reshape_squeeze.43) | copy-start | bytes 903172
  280.5 39.5 %copy-start.175 = (bf16[150,512]{1,0:T(8,128)(2,1)S(1)}, bf16[150,512]{1,0:T(8,128)(2,1)}, u32[]{:S(2)}) copy-start(bf16[150,512]{1,0:T(8,128)(2,1)} %reshape_squeeze.42) | copy-start | bytes 460804
  348.7 68.8 %all-gather.11.cloned.1.call-start = ((), (), s32[]{:S(2)}) async-start(), calls=%async_computation.4 | async-start | bytes 3522560 | tf_op jit(solution)/shard_map/all_gather | solution.py:224
  352.5 288.7 %all-gather.13.cloned.1.call-start = ((), (), s32[]{:S(2)}) async-start(), calls=%async_computation.5 | async-start | bytes 1761280 | tf_op jit(solution)/shard_map/all_gather | solution.py:269
  551.1 19.0 %copy-start.292 = (f32[256]{0:T(256)S(1)}, f32[256]{0:T(256)}, u32[]{:S(2)}) copy-start(f32[256]{0:T(256)} %get-tuple-element.110) | copy-start | bytes 3076
  552.9 20.4 %copy-start.161 = (bf16[294,256]{0,1:T(8,128)(2,1)S(1)}, bf16[294,256]{0,1:T(8,128)(2,1)}, u32[]{:S(2)}) copy-start(bf16[294,256]{0,1:T(8,128)(2,1)} %copy.238) | copy-start | bytes 451588
  552.9 20.4 %copy-start.209 = (bf16[294,8,32]{2,1,0:T(8,128)(2,1)S(1)}, bf16[294,8,32]{2,1,0:T(8,128)(2,1)}, u32[]{:S(2)}) copy-start(bf16[294,8,32]{2,1,0:T(8,128)(2,1)} %reshape.842) | copy-start | bytes 451588
  572.8 72.1 %all-gather.17.cloned.1.call-start = ((), (), s32[]{:S(2)}) async-start(), calls=%async_computation.7 | async-start | bytes 1761280 | tf_op jit(solution)/shard_map/all_gather | solution.py:269
  597.9 210.4 %all-reduce.21.cloned.1.call-start = ((), (), s32[]{:S(2)}) async-start(), calls=%async_computation.8 | async-start | bytes 10747904 | tf_op jit(solution)/shard_map/psum | solution.py:282
  (274 other events, 803.7 us)
Sparse Core Ops, SparseCore 0:
  246.0 24.1 all-gather.6
  271.8 19.8 all-gather.8
  348.8 24.4 all-gather.14
  375.3 26.6 all-gather.10
  573.0 16.6 all-gather.12
  598.1 16.6 all-gather.16
  619.9 188.4 all-reduce.20
